TPU v7x, 32 devices: a whole 2x2x4 slice. The times are simulated.
32 devices in a mesh: dp: 4 (over x, core), seq: 4 (over z), shard: 2 (over y).
Axes of the slice: x: 2, y: 2, z: 4, core: 2. Of those that a mesh axis runs over, the one named last changes fastest.
Arguments:
- layer_input: bfloat16 [8, 2048, 1024], P(('dp', 'shard'), 'seq'), may hold values from -6 to 6
- cond_table: bfloat16 [8, 1024], replicated, may hold values from -3 to 3
- window_bucket: int32 [8], P(('dp', 'shard')), may hold values from 0 to 7, as said below
- window_blocks: int32 [8], P(('dp', 'shard')), may hold values from 1 to 16, as said below
- cotangent: bfloat16 [8, 2048, 1024], P(('dp', 'shard'), 'seq'), may hold values from -6 to 6
- ln1_gain: float32 [1024], P(('dp', 'seq', 'shard')), may hold values from 0.25 to 1.75
- ln1_bias: float32 [1024], P(('dp', 'seq', 'shard')), may hold values from -2 to 2
- qkv_weight: float32 [1024, 3072], P(('dp', 'seq', 'shard')), may hold values from -0.1875 to 0.1875
- query_bias: float32 [1024], P(('dp', 'seq', 'shard')), may hold values from -2 to 2
- value_bias: float32 [1024], P(('dp', 'seq', 'shard')), may hold values from -2 to 2
- out_weight: float32 [1024, 1024], P(('dp', 'seq', 'shard')), may hold values from -0.75 to 0.75
- out_bias: float32 [1024], P(('dp', 'seq', 'shard')), may hold values from -2 to 2
- ln2_gain: float32 [1024], P(('dp', 'seq', 'shard')), may hold values from 0.25 to 1.75
- ln2_bias: float32 [1024], P(('dp', 'seq', 'shard')), may hold values from -2 to 2
- fc_weight: float32 [1024, 4096], P(('dp', 'seq', 'shard')), may hold values from -0.1875 to 0.1875
- fc_bias: float32 [4096], P(('dp', 'seq', 'shard')), may hold values from -2 to 2
- proj_weight: float32 [4096, 1024], P(('dp', 'seq', 'shard')), may hold values from -0.09375 to 0.09375
- proj_bias: float32 [1024], P(('dp', 'seq', 'shard')), may hold values from -2 to 2
Outputs:
- layer_output: bfloat16 [8, 2048, 1024], P(('dp', 'shard'), 'seq')
- input_grad: float32 [8, 2048, 1024], P(('dp', 'shard'), 'seq')
- ln1_gain_grad: float32 [1024], P(('dp', 'seq', 'shard'))
- ln1_bias_grad: float32 [1024], P(('dp', 'seq', 'shard'))
- qkv_weight_grad: float32 [1024, 3072], P(('dp', 'seq', 'shard'))
- query_bias_grad: float32 [1024], P(('dp', 'seq', 'shard'))
- value_bias_grad: float32 [1024], P(('dp', 'seq', 'shard'))
- out_weight_grad: float32 [1024, 1024], P(('dp', 'seq', 'shard'))
- out_bias_grad: float32 [1024], P(('dp', 'seq', 'shard'))
- ln2_gain_grad: float32 [1024], P(('dp', 'seq', 'shard'))
- ln2_bias_grad: float32 [1024], P(('dp', 'seq', 'shard'))
- fc_weight_grad: float32 [1024, 4096], P(('dp', 'seq', 'shard'))
- fc_bias_grad: float32 [4096], P(('dp', 'seq', 'shard'))
- proj_weight_grad: float32 [4096, 1024], P(('dp', 'seq', 'shard'))
- proj_bias_grad: float32 [1024], P(('dp', 'seq', 'shard'))
Inputs may be any that keep to these rules, and one draw needn't show every extreme that they name: `window_bucket`: some window has bucket 0 and some other bucket 8 - 1. `window_blocks`: some window has 16 live rows and some other has 1.
All inputs are finite; a program needn't handle non-finite values.
Results may differ from a plain program's by a relative error of at most 0.012.
The roundings to bfloat16 on the way count: a program that leaves them out, or rounds other values in their place, can miss the bound.
Values may be sent and summed in bfloat16 or wider, within the bound.
A program may use at most 192 MiB of HBM per device.

v0:
```python
import jax
import jax.numpy as jnp
from jax import lax
from jax.sharding import PartitionSpec as P

HEADS = 16
HEAD_DIM = 64
ROW = 128


EPS = 1e-05
MASKED = -1e30


def layer_norm(inputs, gain_row, bias_term):
    center = jnp.mean(inputs, axis=-1, keepdims=True)
    offset = inputs - center
    spread = jnp.mean(offset * offset, axis=-1, keepdims=True)
    return offset * lax.rsqrt(spread + EPS) * gain_row + bias_term


def norm_backward(inputs, gain_row, bias_term, upstream):
    result, pullback = jax.vjp(layer_norm, inputs, gain_row, bias_term)
    return pullback(upstream)


def gelu_tanh(inputs):
    return jax.nn.gelu(inputs, approximate=True)


def column_sum(inputs):
    return jnp.sum(inputs.astype(jnp.float32), axis=0)


def cross_rows(former, latter):
    return lax.dot_general(
        former, latter, (((0,), (0,)), ((), ())), preferred_element_type=jnp.float32
    )


def times_transposed(former, latter):
    return lax.dot_general(
        former, latter, (((1,), (1,)), ((), ())), preferred_element_type=jnp.float32
    )


def split_heads(inputs):
    return inputs.reshape(inputs.shape[0] // ROW, ROW, HEADS, HEAD_DIM)


def block_scores(queries, key_rows):
    factor = HEAD_DIM ** (-0.5)
    scores = (
        jnp.einsum(
            "bqhe,bkhe->bhqk",
            split_heads(queries),
            split_heads(key_rows),
            preferred_element_type=jnp.float32,
        )
        * factor
    )
    places = jnp.arange(ROW, dtype=jnp.int32)
    return jnp.where((places[:, None] >= places[None, :])[None, None], scores, MASKED)


def project(normed, weights, query_add, value_add):
    features = normed.shape[1]
    joined = jnp.dot(normed, weights, preferred_element_type=jnp.float32)
    queries = (joined[:, :features] + query_add).astype(jnp.bfloat16)
    key_rows = joined[:, features : 2 * features].astype(jnp.bfloat16)
    values = (joined[:, 2 * features :] + value_add).astype(jnp.bfloat16)
    return (queries, key_rows, values)


def attention_forward(queries, key_rows, values):
    scores = block_scores(queries, key_rows)
    row_max = jnp.max(scores, axis=-1, keepdims=True)
    powers = jnp.exp(scores - row_max)
    totals = jnp.sum(powers, axis=-1, keepdims=True)
    probs_low = (powers / totals).astype(jnp.bfloat16)
    mixed = jnp.einsum(
        "bhqk,bkhe->bqhe", probs_low, split_heads(values), preferred_element_type=jnp.float32
    )
    return (mixed.reshape(queries.shape).astype(jnp.bfloat16), row_max + jnp.log(totals))


def attention_backward(queries, key_rows, values, log_total, grad_mixed):
    factor = HEAD_DIM ** (-0.5)
    softmax_rows = jnp.exp(block_scores(queries, key_rows) - log_total)
    probs_low = softmax_rows.astype(jnp.bfloat16)
    grad_heads = split_heads(grad_mixed)
    grad_probs = jnp.einsum(
        "bqhe,bkhe->bhqk", grad_heads, split_heads(values), preferred_element_type=jnp.float32
    )
    grad_values = jnp.einsum(
        "bhqk,bqhe->bkhe", probs_low, grad_heads, preferred_element_type=jnp.float32
    )
    weighted = jnp.sum(grad_probs * softmax_rows, axis=-1, keepdims=True)
    grad_scores = (softmax_rows * (grad_probs - weighted)).astype(jnp.bfloat16)
    grad_queries = (
        jnp.einsum(
            "bhqk,bkhe->bqhe",
            grad_scores,
            split_heads(key_rows),
            preferred_element_type=jnp.float32,
        )
        * factor
    )
    grad_keys = (
        jnp.einsum(
            "bhqk,bqhe->bkhe", grad_scores, split_heads(queries), preferred_element_type=jnp.float32
        )
        * factor
    )
    row_shape = queries.shape
    return jnp.concatenate(
        [
            grad_queries.reshape(row_shape),
            grad_keys.reshape(row_shape),
            grad_values.reshape(row_shape),
        ],
        axis=1,
    ).astype(jnp.bfloat16)


def on_device(
    layer_input,
    cond_table,
    window_bucket,
    window_blocks,
    cotangent,
    ln1_gain,
    ln1_bias,
    qkv_weight,
    query_bias,
    value_bias,
    out_weight,
    out_bias,
    ln2_gain,
    ln2_bias,
    fc_weight,
    fc_bias,
    proj_weight,
    proj_bias,
):
    masters = (
        ln1_gain,
        ln1_bias,
        qkv_weight,
        query_bias,
        value_bias,
        out_weight,
        out_bias,
        ln2_gain,
        ln2_bias,
        fc_weight,
        fc_bias,
        proj_weight,
        proj_bias,
    )
    lowered = [member.astype(jnp.bfloat16) for member in masters]
    gathered = (
        lax.all_gather(lowered[0], ("dp", "seq", "shard"), axis=0, tiled=True),
        lax.all_gather(lowered[1], ("dp", "seq", "shard"), axis=0, tiled=True),
        lax.all_gather(lowered[2], ("dp", "seq", "shard"), axis=0, tiled=True),
        lax.all_gather(lowered[3], ("dp", "seq", "shard"), axis=0, tiled=True),
        lax.all_gather(lowered[4], ("dp", "seq", "shard"), axis=0, tiled=True),
        lax.all_gather(lowered[5], ("dp", "seq", "shard"), axis=0, tiled=True),
        lax.all_gather(lowered[6], ("dp", "seq", "shard"), axis=0, tiled=True),
        lax.all_gather(lowered[7], ("dp", "seq", "shard"), axis=0, tiled=True),
        lax.all_gather(lowered[8], ("dp", "seq", "shard"), axis=0, tiled=True),
        lax.all_gather(lowered[9], ("dp", "seq", "shard"), axis=0, tiled=True),
        lax.all_gather(lowered[10], ("dp", "seq", "shard"), axis=0, tiled=True),
        lax.all_gather(lowered[11], ("dp", "seq", "shard"), axis=0, tiled=True),
        lax.all_gather(lowered[12], ("dp", "seq", "shard"), axis=0, tiled=True),
    )
    floats = [member.astype(jnp.float32) for member in gathered]
    windows, window_span, features = layer_input.shape
    buckets = jnp.arange(cond_table.shape[0], dtype=jnp.int32)
    one_hot = (window_bucket[:, None] == buckets[None, :]).astype(jnp.float32)
    cond_rows = jnp.dot(one_hot, cond_table.astype(jnp.float32), precision=lax.Precision.HIGHEST)
    base_rows = (layer_input.astype(jnp.float32) + cond_rows[:, None, :]).reshape(
        windows * window_span, features
    )
    first_normed = layer_norm(base_rows, floats[0], floats[1]).astype(jnp.bfloat16)
    queries, key_rows, values = project(first_normed, gathered[2], floats[3], floats[4])
    mixed_rows, log_total = attention_forward(queries, key_rows, values)
    middle = (
        base_rows + jnp.dot(mixed_rows, gathered[5], preferred_element_type=jnp.float32) + floats[6]
    )
    second_normed = layer_norm(middle, floats[7], floats[8]).astype(jnp.bfloat16)
    hidden_pre = (
        jnp.dot(second_normed, gathered[9], preferred_element_type=jnp.float32) + floats[10]
    )
    hidden = gelu_tanh(hidden_pre).astype(jnp.bfloat16)
    final_rows = (
        middle + jnp.dot(hidden, gathered[11], preferred_element_type=jnp.float32) + floats[12]
    )
    layer_output = final_rows.astype(jnp.bfloat16).reshape(windows, window_span, features)
    back_params = (
        lax.all_gather(lowered[0], ("dp", "seq", "shard"), axis=0, tiled=True),
        lax.all_gather(lowered[1], ("dp", "seq", "shard"), axis=0, tiled=True),
        lax.all_gather(lowered[2], ("dp", "seq", "shard"), axis=0, tiled=True),
        lax.all_gather(lowered[3], ("dp", "seq", "shard"), axis=0, tiled=True),
        lax.all_gather(lowered[4], ("dp", "seq", "shard"), axis=0, tiled=True),
        lax.all_gather(lowered[5], ("dp", "seq", "shard"), axis=0, tiled=True),
        lax.all_gather(lowered[6], ("dp", "seq", "shard"), axis=0, tiled=True),
        lax.all_gather(lowered[7], ("dp", "seq", "shard"), axis=0, tiled=True),
        lax.all_gather(lowered[8], ("dp", "seq", "shard"), axis=0, tiled=True),
        lax.all_gather(lowered[9], ("dp", "seq", "shard"), axis=0, tiled=True),
        lax.all_gather(lowered[10], ("dp", "seq", "shard"), axis=0, tiled=True),
        lax.all_gather(lowered[11], ("dp", "seq", "shard"), axis=0, tiled=True),
        lax.all_gather(lowered[12], ("dp", "seq", "shard"), axis=0, tiled=True),
    )
    back_floats = [member.astype(jnp.float32) for member in back_params]
    first_place = lax.axis_index("seq") * window_span
    places = first_place + jnp.arange(window_span, dtype=jnp.int32)
    keep_mask = (places[None, :] // ROW < window_blocks[:, None]).astype(jnp.float32)
    grad_out = (cotangent.astype(jnp.float32) * keep_mask[:, :, None]).reshape(
        windows * window_span, features
    )
    grad_low = grad_out.astype(jnp.bfloat16)
    proj_w_grad = cross_rows(hidden, grad_low)
    proj_b_grad = column_sum(grad_out)
    grad_hidden = times_transposed(grad_low, back_params[11])
    gelu_value, gelu_pull = jax.vjp(gelu_tanh, hidden_pre)
    grad_pre = gelu_pull(grad_hidden)[0].astype(jnp.bfloat16)
    fc_w_grad = cross_rows(second_normed, grad_pre)
    fc_b_grad = column_sum(grad_pre)
    grad_second = times_transposed(grad_pre, back_params[9])
    grad_middle_norm, ln2_g_grad, ln2_b_grad = norm_backward(
        middle, back_floats[7], back_floats[8], grad_second
    )
    grad_middle = grad_out + grad_middle_norm
    grad_branch = grad_middle.astype(jnp.bfloat16)
    out_w_grad = cross_rows(mixed_rows, grad_branch)
    out_b_grad = column_sum(grad_branch)
    grad_mixed = times_transposed(grad_branch, back_params[5]).astype(jnp.bfloat16)
    again_normed = layer_norm(base_rows, back_floats[0], back_floats[1]).astype(jnp.bfloat16)
    again_queries, again_keys, again_values = project(
        again_normed, back_params[2], back_floats[3], back_floats[4]
    )
    grad_qkv = attention_backward(again_queries, again_keys, again_values, log_total, grad_mixed)
    qkv_w_grad = cross_rows(again_normed, grad_qkv)
    query_b_grad = column_sum(grad_qkv[:, :features])
    value_b_grad = column_sum(grad_qkv[:, 2 * features :])
    grad_first = times_transposed(grad_qkv, back_params[2])
    grad_base_norm, ln1_g_grad, ln1_b_grad = norm_backward(
        base_rows, back_floats[0], back_floats[1], grad_first
    )
    input_grad = (grad_middle + grad_base_norm).reshape(windows, window_span, features)
    shares = (
        lax.psum_scatter(ln1_g_grad, ("dp", "seq", "shard"), scatter_dimension=0, tiled=True),
        lax.psum_scatter(ln1_b_grad, ("dp", "seq", "shard"), scatter_dimension=0, tiled=True),
        lax.psum_scatter(qkv_w_grad, ("dp", "seq", "shard"), scatter_dimension=0, tiled=True),
        lax.psum_scatter(query_b_grad, ("dp", "seq", "shard"), scatter_dimension=0, tiled=True),
        lax.psum_scatter(value_b_grad, ("dp", "seq", "shard"), scatter_dimension=0, tiled=True),
        lax.psum_scatter(out_w_grad, ("dp", "seq", "shard"), scatter_dimension=0, tiled=True),
        lax.psum_scatter(out_b_grad, ("dp", "seq", "shard"), scatter_dimension=0, tiled=True),
        lax.psum_scatter(ln2_g_grad, ("dp", "seq", "shard"), scatter_dimension=0, tiled=True),
        lax.psum_scatter(ln2_b_grad, ("dp", "seq", "shard"), scatter_dimension=0, tiled=True),
        lax.psum_scatter(fc_w_grad, ("dp", "seq", "shard"), scatter_dimension=0, tiled=True),
        lax.psum_scatter(fc_b_grad, ("dp", "seq", "shard"), scatter_dimension=0, tiled=True),
        lax.psum_scatter(proj_w_grad, ("dp", "seq", "shard"), scatter_dimension=0, tiled=True),
        lax.psum_scatter(proj_b_grad, ("dp", "seq", "shard"), scatter_dimension=0, tiled=True),
    )
    return (
        layer_output,
        input_grad,
        shares[0],
        shares[1],
        shares[2],
        shares[3],
        shares[4],
        shares[5],
        shares[6],
        shares[7],
        shares[8],
        shares[9],
        shares[10],
        shares[11],
        shares[12],
    )


def solution(mesh):
    placed = (
        P(("dp", "shard"), "seq", None),
        P(),
        P(("dp", "shard")),
        P(("dp", "shard")),
        P(("dp", "shard"), "seq", None),
        P(("dp", "seq", "shard")),
        P(("dp", "seq", "shard")),
        P(("dp", "seq", "shard"), None),
        P(("dp", "seq", "shard")),
        P(("dp", "seq", "shard")),
        P(("dp", "seq", "shard"), None),
        P(("dp", "seq", "shard")),
        P(("dp", "seq", "shard")),
        P(("dp", "seq", "shard")),
        P(("dp", "seq", "shard"), None),
        P(("dp", "seq", "shard")),
        P(("dp", "seq", "shard"), None),
        P(("dp", "seq", "shard")),
    )
    return jax.shard_map(
        on_device,
        mesh=mesh,
        in_specs=placed,
        out_specs=(
            P(("dp", "shard"), "seq", None),
            P(("dp", "shard"), "seq", None),
            P(("dp", "seq", "shard")),
            P(("dp", "seq", "shard")),
            P(("dp", "seq", "shard"), None),
            P(("dp", "seq", "shard")),
            P(("dp", "seq", "shard")),
            P(("dp", "seq", "shard"), None),
            P(("dp", "seq", "shard")),
            P(("dp", "seq", "shard")),
            P(("dp", "seq", "shard")),
            P(("dp", "seq", "shard"), None),
            P(("dp", "seq", "shard")),
            P(("dp", "seq", "shard"), None),
            P(("dp", "seq", "shard")),
        ),
        check_vma=False,
    )
```

profile of v0, /device:TPU:0, one launch (start us, length us, event | category | flops | bytes accessed | tf_op | source)
XLA Modules:
  0.0 1356.8 jit_solution(13282271950915478034)
XLA Ops:
  7.4 1.8 convert_element_type.160
  9.3 1.5 convert_element_type.171
  10.9 1.8 convert_element_type.179
  12.7 0.7 convert_element_type.183
  16.7 42.5 %all-reduce.18 = (bf16[1024]{0:T(1024)(128)(2,1)S(1)}, bf16[1024]{0:T(1024)(128)(2,1)S(1)}, bf16[1024]{0:T(1024)(128)(2,1)S(1)}, bf16[1024]{0:T(1024)(128)(2,1)S...) all-reduce(bf16[1024]{0:T(1024)(128)(2,1)S(1)} %dynamic-update-slic, ...), channel_id=1, replica_groups=mesh['dp'=4,'seq'=4,'shard'=2] {'dp','seq','shard'}, use_global_device_ids=true, to_apply=%add.4 | all-reduce | flops 8192 | bytes 32768
  59.3 66.3 %all-gather = bf16[32,1,128]{2,1,0:T(2,128)(2,1)S(1)} all-gather(bf16[1,1,128]{2,1,0:T(2,128)(2,1)S(1)} %convert_bitcast_fusion), channel_id=1, replica_groups=mesh['dp'=4,'seq'=4,'shard'=2] {'dp','seq','shard'}, dimensions={0}, use_global_device_ids=true | all-gather | bytes 8448 | tf_op jit(solution)/shard_map/all_gather | solution.py:173
  126.6 6.0 fusion.51
  132.8 1.6 fusion.11
  134.3 2.3 reshape.257
  136.6 2.8 copy.68
  139.5 2.3 reshape.258
  141.8 2.8 copy.69
  144.6 4.3 reshape.256
  149.0 3.5 copy.70
  152.5 1.0 fusion.58
  153.5 1.0 fusion.7
  154.5 0.9 copy-done.2
  155.5 0.8 fusion.23
  156.3 1.9 copy.72
  158.2 3.3 fusion.59
  161.9 60.0 %all-gather.10.cloned.1.call-done = bf16[1024,4096]{1,0:T(8,128)(2,1)} async-done(((bf16[32,4096]{1,0:T(8,128)(2,1)}), bf16[1024,4096]{1,0:T(8,128)(2,1)}) %all-gather.10.cloned.1.call-update) | async-done | bytes 8388624 | tf_op jit(solution)/shard_map/all_gather | solution.py:172
  221.9 10.6 fusion.54
  232.5 68.5 %all-gather.12.cloned.1.call-done = bf16[4096,1024]{1,0:T(8,128)(2,1)} async-done(((bf16[128,1024]{1,0:T(8,128)(2,1)}), bf16[4096,1024]{1,0:T(8,128)(2,1)}) %all-gather.12.cloned.1.call-update) | async-done | bytes 8388624 | tf_op jit(solution)/shard_map/all_gather | solution.py:174
  301.0 13.5 convert_reduce_fusion
  314.5 5.0 multiply_reduce_fusion.1
  319.5 0.7 fusion.57
  321.5 1.0 copy-done.19
  322.5 3.3 fusion.31
  326.0 4.2 convolution_convert_fusion
  330.1 4.2 reshape.259
  334.4 3.6 copy.74
  337.9 4.2 fusion.24
  342.2 0.9 copy.84
  343.7 1.2 multiply_reduce_fusion
  344.9 1.3 multiply_convert_fusion.1
  346.2 0.7 fusion.27
  346.9 0.9 copy.78
  348.1 1.5 fusion.28
  349.6 0.9 copy.81
  351.0 1.8 copy-done.21
  352.9 6.8 fusion.50
  360.0 15.9 %fusion.36 = f32[4096,1024]{1,0:T(8,128)} fusion(bf16[1,512,1024]{2,1,0:T(8,128)(2,1)} %param.22, f32[512]{0:T(512)S(1)} %fusion.42, f32[512,4096]{1,0:T(8,128)} %fusion.54, f32[4096]{0:T(1024)S(1)} %bitcast.132), kind=kOutput, calls=%fused_computation.71 | convolution fusion | flops 4317511680 | bytes 26232832 | tf_op jit(solution)/shard_map/dot_general | solution.py:36
  376.2 10.5 fusion.53
  386.8 1.6 fusion.15
  388.4 1.4 convert_reduce_fusion.2
  390.1 7.0 fusion.55
  397.1 1.3 copy-done.15
  398.4 1.0 multiply_reduce_fusion.2
  399.4 42.3 %all-reduce.17 = (f32[1024]{0:T(1024)S(1)}, f32[1024]{0:T(1024)S(1)}, f32[1024]{0:T(1024)S(1)}, f32[1024]{0:T(1024)S(1)}, f32[1024]{0:T(1024)S(1)}, /*index=5*/f...) all-reduce(f32[1024]{0:T(1024)S(1)} %get-tuple-element.17, ...), channel_id=2, replica_groups=mesh['dp'=4,'seq'=4,'shard'=2] {'dp','seq','shard'}, use_global_device_ids=true, to_apply=%region_12.13.clone | all-reduce | flops 12288 | bytes 98304
  441.8 0.6 dynamic-slice
  442.4 0.6 dynamic-slice.1
  442.9 0.6 dynamic-slice.2
  443.5 0.6 dynamic-slice.3
  444.1 0.6 dynamic-slice.4
  444.7 0.6 dynamic-slice.5
  445.3 0.6 dynamic-slice.6
  445.9 0.6 dynamic-slice.8
  446.4 0.6 dynamic-slice.7
  447.0 4.1 add_bitcast_fusion
  451.1 12.3 fusion.29
  463.4 6.8 reduce-scatter.7.cloned.1.call-done
  470.2 159.2 %reduce-scatter.5.cloned.1.call-done = f32[32,3072]{1,0:T(8,128)} async-done(((f32[1024,3072]{1,0:T(8,128)}), f32[32,3072]{1,0:T(8,128)}) %reduce-scatter.5.cloned.1.call-update) | async-done | bytes 393232 | tf_op jit(solution)/shard_map/reduce_scatter | solution.py:255
  629.4 360.0 %reduce-scatter.11.cloned.1.call-done = f32[128,1024]{1,0:T(8,128)} async-done(((f32[4096,1024]{1,0:T(8,128)}), f32[128,1024]{1,0:T(8,128)}) %reduce-scatter.11.cloned.1.call-update) | async-done | bytes 524304 | tf_op jit(solution)/shard_map/reduce_scatter | solution.py:264
  989.4 360.2 %reduce-scatter.9.cloned.1.call-done = f32[32,4096]{1,0:T(8,128)} async-done(((f32[1024,4096]{1,0:T(8,128)}), f32[32,4096]{1,0:T(8,128)}) %reduce-scatter.9.cloned.1.call-update) | async-done | bytes 524304 | tf_op jit(solution)/shard_map/reduce_scatter | solution.py:262
  (135 shorter events, 7.3 us)
Async XLA Ops:
  7.2 118.5 %copy-start = (bf16[8,1024]{1,0:T(8,128)(2,1)S(1)}, bf16[8,1024]{1,0:T(8,128)(2,1)}, u32[]{:S(2)}) copy-start(bf16[8,1024]{1,0:T(8,128)(2,1)} %param.19) | copy-start | bytes 49156
  7.2 5.5 copy-start.20
  7.2 7.6 copy-start.23
  7.2 7.6 copy-start.24
  7.2 7.7 copy-start.25
  7.2 7.7 copy-start.26
  7.3 7.7 copy-start.27
  7.3 7.7 copy-start.28
  7.3 7.7 copy-start.29
  7.3 7.7 copy-start.30
  7.3 52.0 %copy-start.31 = (f32[128]{0:T(128)S(1)}, f32[128]{0:T(128)}, u32[]{:S(2)}) copy-start(f32[128]{0:T(128)} %param.33) | copy-start | bytes 1540
  7.3 118.5 %copy-start.4 = (bf16[1,512,1024]{2,1,0:T(8,128)(2,1)S(1)}, bf16[1,512,1024]{2,1,0:T(8,128)(2,1)}, u32[]{:S(2)}) copy-start(bf16[1,512,1024]{2,1,0:T(8,128)(2,1)} %param.18) | copy-start | bytes 3145732
  7.3 119.3 %all-gather.6.cloned.1.call-start = ((), (), s32[]{:S(2)}) async-start(), calls=%async_computation.4 | async-start | bytes 6488064 | tf_op jit(solution)/shard_map/all_gather | solution.py:165
  9.2 149.0 %all-gather.8.cloned.1.call-start = ((), (), s32[]{:S(2)}) async-start(), calls=%async_computation.5 | async-start | bytes 2162688 | tf_op jit(solution)/shard_map/all_gather | solution.py:168
  10.8 211.0 %all-gather.10.cloned.1.call-start = ((), (), s32[]{:S(2)}) async-start(), calls=%async_computation.6 | async-start | bytes 8650752 | tf_op jit(solution)/shard_map/all_gather | solution.py:172
  12.7 288.3 %all-gather.12.cloned.1.call-start = ((), (), s32[]{:S(2)}) async-start(), calls=%async_computation.7 | async-start | bytes 8650752 | tf_op jit(solution)/shard_map/all_gather | solution.py:174
  13.5 456.7 %reduce-scatter.7.cloned.1.call-start = ((), (), s32[]{:S(2)}) async-start(), calls=%async_computation.9 | async-start | bytes 4325376 | tf_op jit(solution)/shard_map/reduce_scatter | solution.py:258
  139.5 13.0 copy-start.10
  144.6 7.8 copy-start.12
  153.5 2.0 copy-start.2
  153.5 2.0 copy-start.16
  301.0 13.5 copy-start.22
  314.5 5.0 copy-start.32
  319.5 1.2 copy-start.14
  320.2 1.3 copy-start.5
  320.7 1.8 copy-start.18
  321.5 1.0 copy-start.19
  325.9 303.5 %reduce-scatter.5.cloned.1.call-start = ((), (), s32[]{:S(2)}) async-start(), calls=%async_computation.8 | async-start | bytes 12976128 | tf_op jit(solution)/shard_map/reduce_scatter | solution.py:255
  337.9 5.1 copy-start.3
  342.2 1.2 copy-start.6
  342.2 1.5 copy-start.17
  343.7 7.2 copy-start.7
  344.9 1.3 copy-start.13
  346.9 1.2 copy-start.11
  348.1 2.4 copy-start.8
  351.0 1.8 copy-start.21
  359.7 629.7 %reduce-scatter.11.cloned.1.call-start = ((), (), s32[]{:S(2)}) async-start(), calls=%async_computation.11 | async-start | bytes 17301504 | tf_op jit(solution)/shard_map/reduce_scatter | solution.py:264
  375.9 973.7 %reduce-scatter.9.cloned.1.call-start = ((), (), s32[]{:S(2)}) async-start(), calls=%async_computation.10 | async-start | bytes 17301504 | tf_op jit(solution)/shard_map/reduce_scatter | solution.py:262
  386.8 3.1 copy-start.9
  397.0 1.4 copy-start.15
  451.1 898.6 %copy-start.1 = (bf16[8,1024]{1,0:T(8,128)(2,1)S(1)}, bf16[8,1024]{1,0:T(8,128)(2,1)}, u32[]{:S(2)}) copy-start(bf16[8,1024]{1,0:T(8,128)(2,1)} %param.19) | copy-start | bytes 49156
Sparse Core Ops, SparseCore 0:
  11.6 72.2 all-gather.5
  87.4 54.8 all-gather.7
  145.9 75.9 all-gather.9
  225.3 75.6 all-gather.11
  326.0 144.1 reduce-scatter.6
  476.6 152.7 reduce-scatter.4
  632.3 357.1 reduce-scatter.10
  992.3 357.3 reduce-scatter.8
where the time goes:
time: 1360 us
  waiting for transfers between devices  1010 us (74%)
  blocking collectives  151 us (11%)
  matrix products  108 us (8%)
  local copies, waits for them, and re-layouts  45 us (3%)
  other arithmetic  20.5 us (2%)
  between operations  16.5 us (1%)
    reduce_scatter x1, waiting for transfers between devices, on_device(): lax.psum_scatter(fc_w_grad, ('dp', 'seq', 'shard'), scatter_dimension=0,...  360 us
    reduce_scatter x1, waiting for transfers between devices, on_device(): lax.psum_scatter(proj_w_grad, ('dp', 'seq', 'shard'), scatter_dimension=0...  360 us
    reduce_scatter x1, waiting for transfers between devices, on_device(): lax.psum_scatter(qkv_w_grad, ('dp', 'seq', 'shard'), scatter_dimension=0,...  159 us
    unnamed x2, blocking collectives  84.9 us
    all_gather x1, waiting for transfers between devices, on_device(): lax.all_gather(lowered[11], ('dp', 'seq', 'shard'), axis=0, tiled=True)  68.5 us
    all_gather x1, blocking collectives, on_device(): lax.all_gather(lowered[10], ('dp', 'seq', 'shard'), axis=0, tiled=True)  66.3 us
    all_gather x1, waiting for transfers between devices, on_device(): lax.all_gather(lowered[9], ('dp', 'seq', 'shard'), axis=0, tiled=True)  60 us
    dot_general x4, matrix products, cross_rows(): lax.dot_general(former, latter, (((0,), (0,)), ((), ())), preferred_eleme...  36.6 us
  transfers between devices with their start and end apart: 8, of which 6 were waited for; matrix products, arithmetic and copies ran while one was open for 10% of the time, Pallas kernels for 0%

commit v1 on v0

--- a/solution.py
+++ b/solution.py
@@ -121,6 +121,46 @@
         ],
         axis=1,
     ).astype(jnp.bfloat16)
+
+
+AXES = ("dp", "seq", "shard")
+
+
+def gather_all(members):
+    devices = lax.psum(1, AXES)
+    flat = jnp.concatenate([member for member in members if member.ndim == 1])
+    joined = lax.all_gather(flat, AXES, axis=0, tiled=False)
+    results = []
+    start = 0
+    for member in members:
+        if member.ndim == 1:
+            size = member.shape[0]
+            results.append(joined[:, start : start + size].reshape(devices * size))
+            start += size
+        else:
+            results.append(lax.all_gather(member, AXES, axis=0, tiled=True))
+    return tuple(results)
+
+
+def scatter_all(members):
+    devices = lax.psum(1, AXES)
+    flat = jnp.concatenate(
+        [member.reshape(devices, -1) for member in members if member.ndim == 1], axis=1
+    )
+    summed = lax.psum_scatter(flat, AXES, scatter_dimension=0, tiled=False)
+    results = []
+    start = 0
+    for member in members:
+        if member.ndim == 1:
+            size = member.shape[0] // devices
+            results.append(summed[start : start + size])
+            start += size
+        else:
+            share = lax.psum_scatter(
+                member.astype(jnp.bfloat16), AXES, scatter_dimension=0, tiled=True
+            )
+            results.append(share.astype(jnp.float32))
+    return tuple(results)
 
 
 def on_device(
@@ -159,21 +199,7 @@
         proj_bias,
     )
     lowered = [member.astype(jnp.bfloat16) for member in masters]
-    gathered = (
-        lax.all_gather(lowered[0], ("dp", "seq", "shard"), axis=0, tiled=True),
-        lax.all_gather(lowered[1], ("dp", "seq", "shard"), axis=0, tiled=True),
-        lax.all_gather(lowered[2], ("dp", "seq", "shard"), axis=0, tiled=True),
-        lax.all_gather(lowered[3], ("dp", "seq", "shard"), axis=0, tiled=True),
-        lax.all_gather(lowered[4], ("dp", "seq", "shard"), axis=0, tiled=True),
-        lax.all_gather(lowered[5], ("dp", "seq", "shard"), axis=0, tiled=True),
-        lax.all_gather(lowered[6], ("dp", "seq", "shard"), axis=0, tiled=True),
-        lax.all_gather(lowered[7], ("dp", "seq", "shard"), axis=0, tiled=True),
-        lax.all_gather(lowered[8], ("dp", "seq", "shard"), axis=0, tiled=True),
-        lax.all_gather(lowered[9], ("dp", "seq", "shard"), axis=0, tiled=True),
-        lax.all_gather(lowered[10], ("dp", "seq", "shard"), axis=0, tiled=True),
-        lax.all_gather(lowered[11], ("dp", "seq", "shard"), axis=0, tiled=True),
-        lax.all_gather(lowered[12], ("dp", "seq", "shard"), axis=0, tiled=True),
-    )
+    gathered = gather_all(lowered)
     floats = [member.astype(jnp.float32) for member in gathered]
     windows, window_span, features = layer_input.shape
     buckets = jnp.arange(cond_table.shape[0], dtype=jnp.int32)
@@ -197,21 +223,7 @@
         middle + jnp.dot(hidden, gathered[11], preferred_element_type=jnp.float32) + floats[12]
     )
     layer_output = final_rows.astype(jnp.bfloat16).reshape(windows, window_span, features)
-    back_params = (
-        lax.all_gather(lowered[0], ("dp", "seq", "shard"), axis=0, tiled=True),
-        lax.all_gather(lowered[1], ("dp", "seq", "shard"), axis=0, tiled=True),
-        lax.all_gather(lowered[2], ("dp", "seq", "shard"), axis=0, tiled=True),
-        lax.all_gather(lowered[3], ("dp", "seq", "shard"), axis=0, tiled=True),
-        lax.all_gather(lowered[4], ("dp", "seq", "shard"), axis=0, tiled=True),
-        lax.all_gather(lowered[5], ("dp", "seq", "shard"), axis=0, tiled=True),
-        lax.all_gather(lowered[6], ("dp", "seq", "shard"), axis=0, tiled=True),
-        lax.all_gather(lowered[7], ("dp", "seq", "shard"), axis=0, tiled=True),
-        lax.all_gather(lowered[8], ("dp", "seq", "shard"), axis=0, tiled=True),
-        lax.all_gather(lowered[9], ("dp", "seq", "shard"), axis=0, tiled=True),
-        lax.all_gather(lowered[10], ("dp", "seq", "shard"), axis=0, tiled=True),
-        lax.all_gather(lowered[11], ("dp", "seq", "shard"), axis=0, tiled=True),
-        lax.all_gather(lowered[12], ("dp", "seq", "shard"), axis=0, tiled=True),
-    )
+    back_params = gathered
     back_floats = [member.astype(jnp.float32) for member in back_params]
     first_place = lax.axis_index("seq") * window_span
     places = first_place + jnp.arange(window_span, dtype=jnp.int32)
@@ -249,20 +261,22 @@
         base_rows, back_floats[0], back_floats[1], grad_first
     )
     input_grad = (grad_middle + grad_base_norm).reshape(windows, window_span, features)
-    shares = (
-        lax.psum_scatter(ln1_g_grad, ("dp", "seq", "shard"), scatter_dimension=0, tiled=True),
-        lax.psum_scatter(ln1_b_grad, ("dp", "seq", "shard"), scatter_dimension=0, tiled=True),
-        lax.psum_scatter(qkv_w_grad, ("dp", "seq", "shard"), scatter_dimension=0, tiled=True),
-        lax.psum_scatter(query_b_grad, ("dp", "seq", "shard"), scatter_dimension=0, tiled=True),
-        lax.psum_scatter(value_b_grad, ("dp", "seq", "shard"), scatter_dimension=0, tiled=True),
-        lax.psum_scatter(out_w_grad, ("dp", "seq", "shard"), scatter_dimension=0, tiled=True),
-        lax.psum_scatter(out_b_grad, ("dp", "seq", "shard"), scatter_dimension=0, tiled=True),
-        lax.psum_scatter(ln2_g_grad, ("dp", "seq", "shard"), scatter_dimension=0, tiled=True),
-        lax.psum_scatter(ln2_b_grad, ("dp", "seq", "shard"), scatter_dimension=0, tiled=True),
-        lax.psum_scatter(fc_w_grad, ("dp", "seq", "shard"), scatter_dimension=0, tiled=True),
-        lax.psum_scatter(fc_b_grad, ("dp", "seq", "shard"), scatter_dimension=0, tiled=True),
-        lax.psum_scatter(proj_w_grad, ("dp", "seq", "shard"), scatter_dimension=0, tiled=True),
-        lax.psum_scatter(proj_b_grad, ("dp", "seq", "shard"), scatter_dimension=0, tiled=True),
+    shares = scatter_all(
+        (
+            ln1_g_grad,
+            ln1_b_grad,
+            qkv_w_grad,
+            query_b_grad,
+            value_b_grad,
+            out_w_grad,
+            out_b_grad,
+            ln2_g_grad,
+            ln2_b_grad,
+            fc_w_grad,
+            fc_b_grad,
+            proj_w_grad,
+            proj_b_grad,
+        )
     )
     return (
         layer_output,

time: 1360 us -> 972 us (0.71)
  waiting for transfers between devices: 1010 us -> 662 us
  blocking collectives: 151 us -> 111 us
    reduce_scatter x4, waiting for transfers between devices: 886 us -> 494 us  [scatter_all(): lax.psum_scatter(member.astype(jnp.bfloat16), AXES, scatter_dimension=0,...]
    unnamed x2 -> x1, blocking collectives: 84.9 us -> 40.3 us
    all_gather x4, waiting for transfers between devices: 129 us -> 168 us  [gather_all(): results.append(lax.all_gather(member, AXES, axis=0, tiled=True))]
  transfers between devices with their start and end apart: 8 -> 8, of which waited for: 6 -> 7; matrix products, arithmetic and copies ran while one was open for 10% -> 14% of each run, Pallas kernels for 0% -> 0%
where the time goes in v1:
time: 972 us; the launch traced here: 962 us
  waiting for transfers between devices  662 us (68%)
  blocking collectives  111 us (11%)
  matrix products  103 us (11%)
  local copies, waits for them, and re-layouts  40.4 us (4%)
  other arithmetic  28.6 us (3%)
  between operations  16.6 us (2%)
    reduce_scatter x4, waiting for transfers between devices, scatter_all(): lax.psum_scatter(member.astype(jnp.bfloat16), AXES, scatter_dimension=0,...  494 us
    all_gather x4, waiting for transfers between devices, gather_all(): results.append(lax.all_gather(member, AXES, axis=0, tiled=True))  168 us
    all_gather x1, blocking collectives, gather_all(): joined = lax.all_gather(flat, AXES, axis=0, tiled=False)  71 us
    unnamed x1, blocking collectives  40.3 us
    dot_general x4, matrix products, cross_rows(): lax.dot_general(former, latter, (((0,), (0,)), ((), ())), preferred_eleme...  31.8 us
    dot_general x4, matrix products, times_transposed(): lax.dot_general(former, latter, (((1,), (1,)), ((), ())), preferred_eleme...  29.6 us
    reshape x8, local copies, waits for them, and re-layouts, split_heads(): return inputs.reshape(inputs.shape[0] // ROW, ROW, HEADS, HEAD_DIM)  25.8 us
  transfers between devices with their start and end apart: 8, of which 7 were waited for; matrix products, arithmetic and copies ran while one was open for 14% of the time, Pallas kernels for 0%

profile of v1, /device:TPU:0, one launch (start us, length us, event | category | flops | bytes accessed | tf_op | source)
XLA Modules:
  0.0 961.9 jit_solution(1778922042258475580)
XLA Ops:
  7.4 1.8 convert_element_type.256
  9.3 1.5 convert_element_type.267
  10.9 1.8 convert_element_type.275
  12.7 0.7 convert_element_type.279
  15.1 71.0 %all-gather.1 = bf16[32,1,384]{2,1,0:T(2,128)(2,1)S(1)} all-gather(bf16[1,1,384]{2,1,0:T(2,128)(2,1)S(1)} %reshape.357), channel_id=2, replica_groups=mesh['dp'=4,'seq'=4,'shard'=2] {'dp','seq','shard'}, dimensions={0}, use_global_device_ids=true | all-gather | bytes 25344 | tf_op jit(solution)/shard_map/all_gather | solution.py:132
  87.7 5.7 fusion.49
  93.6 1.6 fusion.11
  95.2 2.3 reshape.363
  97.5 2.8 copy.68
  100.3 2.3 reshape.364
  102.6 2.8 copy.69
  105.5 4.3 reshape.362
  109.8 3.5 copy.70
  113.3 1.0 fusion.55
  114.3 1.0 fusion.7
  115.3 0.9 copy-done.2
  116.3 0.8 fusion.23
  117.1 1.9 copy.72
  119.1 23.2 %all-gather.9.cloned.1.call-done = bf16[1024,1024]{1,0:T(8,128)(2,1)} async-done(((bf16[32,1024]{1,0:T(8,128)(2,1)}), bf16[1024,1024]{1,0:T(8,128)(2,1)}) %all-gather.9.cloned.1.call-update) | async-done | bytes 2097168 | tf_op jit(solution)/shard_map/all_gather | solution.py:141
  142.3 3.3 fusion.56
  146.0 75.8 %all-gather.11.cloned.1.call-done = bf16[1024,4096]{1,0:T(8,128)(2,1)} async-done(((bf16[32,4096]{1,0:T(8,128)(2,1)}), bf16[1024,4096]{1,0:T(8,128)(2,1)}) %all-gather.11.cloned.1.call-update) | async-done | bytes 8388624 | tf_op jit(solution)/shard_map/all_gather | solution.py:141
  221.8 10.6 %fusion.51 = f32[512,4096]{1,0:T(8,128)} fusion(bf16[1024,4096]{1,0:T(8,128)(2,1)} %all-gather.11.cloned.1.call-done, f32[512,1024]{1,0:T(8,128)S(1)} %get-tuple-element.47, f32[1024]{0:T(1024)S(1)} %reshape.353, f32[1024]{0:T(1024)S(1)} %reshape.352, f32[512]{0:T(512)S(1)} %fusion.46, f32[512]{0:T(512)S(1)} %broadcast_multiply_fusion), kind=kOutput, calls=%fused_computation.125 | convolution fusion | flops 4297588736 | bytes 18886656 | tf_op jit(solution)/shard_map/dot_general | solution.py:219
  232.5 68.5 %all-gather.13.cloned.1.call-done = bf16[4096,1024]{1,0:T(8,128)(2,1)} async-done(((bf16[128,1024]{1,0:T(8,128)(2,1)}), bf16[4096,1024]{1,0:T(8,128)(2,1)}) %all-gather.13.cloned.1.call-update) | async-done | bytes 8388624 | tf_op jit(solution)/shard_map/all_gather | solution.py:141
  301.0 13.5 %convert_reduce_fusion = (f32[4096]{0:T(1024)S(1)}, bf16[512,4096]{1,0:T(8,128)(2,1)S(1)}) fusion(f32[512,4096]{1,0:T(8,128)} %fusion.51, f32[4096]{0:T(1024)S(1)} %fusion.36, bf16[4096,1024]{1,0:T(8,128)(2,1)} %all-gather.13.cloned.1.call-done, bf16[1,512,1024]{2,1,0:T(8,128)(2,1)} %param.22, f32[512]{0:T(512)S(1)} %fusion.41), kind=kOutput, calls=%fused_computation.9 | convolution fusion | flops 4344770560 | bytes 22054912 | tf_op jit(solution)/shard_map/dot_general | solution.py:42
  314.5 5.0 multiply_reduce_fusion.1
  319.5 0.7 fusion.54
  320.2 0.5 copy-done.13
  320.7 0.4 convert_reduce_fusion.1
  321.5 1.0 copy-done.18
  322.5 2.6 convolution_convert_fusion.3
  325.2 4.2 convolution_convert_fusion.4
  329.4 4.2 reshape.365
  333.6 3.5 copy.74
  337.1 4.2 fusion.24
  341.4 0.9 copy.84
  342.9 1.2 multiply_reduce_fusion
  344.1 1.3 multiply_convert_fusion.1
  345.4 0.7 fusion.27
  346.1 0.9 copy.78
  347.3 1.5 fusion.28
  348.8 0.9 copy.81
  350.2 1.6 copy-done.20
  351.8 6.2 convolution_convert_fusion.2
  358.1 13.5 %convolution_convert_fusion = bf16[4096,1024]{1,0:T(8,128)(2,1)} fusion(bf16[1,512,1024]{2,1,0:T(8,128)(2,1)} %param.22, f32[512]{0:T(512)S(1)} %fusion.41, f32[512,4096]{1,0:T(8,128)} %fusion.51, f32[4096]{0:T(1024)S(1)} %fusion.36), kind=kOutput, calls=%fused_computation.11 | convolution fusion | flops 4321705984 | bytes 17844224 | tf_op jit(solution)/shard_map/dot_general | solution.py:36
  371.7 9.5 convolution_convert_fusion.1
  381.2 1.5 fusion.15
  383.1 1.4 convert_reduce_fusion.2
  384.6 1.4 convert_reduce_fusion.3
  386.1 6.9 fusion.52
  393.1 1.3 copy-done.14
  394.4 1.0 multiply_reduce_fusion.2
  395.7 40.3 %all-reduce = f32[32,384]{1,0:T(8,128)S(1)} all-reduce(f32[32,384]{1,0:T(8,128)S(1)} %concatenate.12), channel_id=3, replica_groups=mesh['dp'=4,'seq'=4,'shard'=2] {'dp','seq','shard'}, use_global_device_ids=true, to_apply=%region_20.21.clone | all-reduce | flops 12288 | bytes 98304
  436.0 0.6 dynamic-slice_bitcast_fusion.1
  436.6 0.6 dynamic-slice_bitcast_fusion
  437.2 4.1 add_bitcast_fusion
  441.3 12.2 %fusion.29 = bf16[1,512,1024]{2,1,0:T(8,128)(2,1)} fusion(f32[512,1024]{1,0:T(8,128)S(1)} %get-tuple-element.47, bf16[4096,1024]{1,0:T(8,128)(2,1)} %all-gather.13.cloned.1.call-done, f32[1024]{0:T(1024)S(1)} %reshape.355, f32[512,4096]{1,0:T(8,128)} %fusion.51, f32[4096]{0:T(1024)S(1)} %fusion.36), kind=kOutput, calls=%fused_computation.65 | convolution fusion | flops 4317511680 | bytes 19943424 | tf_op jit(solution)/shard_map/dot_general | solution.py:223
  453.5 10.2 %reduce-scatter.7.cloned.1.call-done = bf16[32,1024]{1,0:T(8,128)(2,1)} async-done(((bf16[1024,1024]{1,0:T(8,128)(2,1)}), bf16[32,1024]{1,0:T(8,128)(2,1)}) %reduce-scatter.7.cloned.1.call-update) | async-done | bytes 65552 | tf_op jit(solution)/shard_map/reduce_scatter | solution.py:159
  463.7 1.5 convert_element_type.298
  465.2 115.6 %reduce-scatter.5.cloned.1.call-done = bf16[32,3072]{1,0:T(8,128)(2,1)} async-done(((bf16[1024,3072]{1,0:T(8,128)(2,1)}), bf16[32,3072]{1,0:T(8,128)(2,1)}) %reduce-scatter.5.cloned.1.call-update) | async-done | bytes 196624 | tf_op jit(solution)/shard_map/reduce_scatter | solution.py:159
  580.8 1.7 convert_element_type.296
  582.5 183.9 %reduce-scatter.11.cloned.1.call-done = bf16[128,1024]{1,0:T(8,128)(2,1)} async-done(((bf16[4096,1024]{1,0:T(8,128)(2,1)}), bf16[128,1024]{1,0:T(8,128)(2,1)}) %reduce-scatter.11.cloned.1.call-update) | async-done | bytes 262160 | tf_op jit(solution)/shard_map/reduce_scatter | solution.py:159
  766.4 1.8 convert_element_type.302
  768.2 184.6 %reduce-scatter.9.cloned.1.call-done = bf16[32,4096]{1,0:T(8,128)(2,1)} async-done(((bf16[1024,4096]{1,0:T(8,128)(2,1)}), bf16[32,4096]{1,0:T(8,128)(2,1)}) %reduce-scatter.9.cloned.1.call-update) | async-done | bytes 262160 | tf_op jit(solution)/shard_map/reduce_scatter | solution.py:159
  952.8 1.8 convert_element_type.300
  (126 shorter events, 5.4 us)
Async XLA Ops:
  7.2 79.6 %copy-start = (bf16[8,1024]{1,0:T(8,128)(2,1)S(1)}, bf16[8,1024]{1,0:T(8,128)(2,1)}, u32[]{:S(2)}) copy-start(bf16[8,1024]{1,0:T(8,128)(2,1)} %param.19) | copy-start | bytes 49156
  7.2 5.5 copy-start.19
  7.2 7.6 copy-start.22
  7.2 7.6 copy-start.23
  7.2 7.7 copy-start.24
  7.2 7.7 copy-start.25
  7.3 7.7 copy-start.26
  7.3 7.7 copy-start.27
  7.3 7.7 copy-start.28
  7.3 7.7 copy-start.29
  7.3 7.7 copy-start.30
  7.3 79.6 %copy-start.4 = (bf16[1,512,1024]{2,1,0:T(8,128)(2,1)S(1)}, bf16[1,512,1024]{2,1,0:T(8,128)(2,1)}, u32[]{:S(2)}) copy-start(bf16[1,512,1024]{2,1,0:T(8,128)(2,1)} %param.18) | copy-start | bytes 3145732
  7.3 80.4 %all-gather.7.cloned.1.call-start = ((), (), s32[]{:S(2)}) async-start(), calls=%async_computation.4 | async-start | bytes 6488064 | tf_op jit(solution)/shard_map/all_gather | solution.py:141
  9.2 133.1 %all-gather.9.cloned.1.call-start = ((), (), s32[]{:S(2)}) async-start(), calls=%async_computation.5 | async-start | bytes 2162688 | tf_op jit(solution)/shard_map/all_gather | solution.py:141
  10.8 211.0 %all-gather.11.cloned.1.call-start = ((), (), s32[]{:S(2)}) async-start(), calls=%async_computation.6 | async-start | bytes 8650752 | tf_op jit(solution)/shard_map/all_gather | solution.py:141
  12.7 288.3 %all-gather.13.cloned.1.call-start = ((), (), s32[]{:S(2)}) async-start(), calls=%async_computation.7 | async-start | bytes 8650752 | tf_op jit(solution)/shard_map/all_gather | solution.py:141
  13.5 450.2 %reduce-scatter.7.cloned.1.call-start = ((), (), s32[]{:S(2)}) async-start(), calls=%async_computation.9 | async-start | bytes 2162688 | tf_op jit(solution)/shard_map/reduce_scatter | solution.py:159
  100.3 13.0 %copy-start.9 = (bf16[4,128,16,64]{1,3,2,0:T(8,128)(2,1)}, bf16[4,128,16,64]{1,3,2,0:T(8,128)(2,1)S(1)}, u32[]{:S(2)}) copy-start(bf16[4,128,16,64]{1,3,2,0:T(8,128)(2,1)S(1)} %copy.68) | copy-start | bytes 3145732
  105.5 7.9 copy-start.11
  114.3 2.0 copy-start.2
  114.3 2.0 copy-start.15
  301.0 13.5 %copy-start.21 = (bf16[1024,4096]{1,0:T(8,128)(2,1)S(1)}, bf16[1024,4096]{1,0:T(8,128)(2,1)}, u32[]{:S(2)}) copy-start(bf16[1024,4096]{1,0:T(8,128)(2,1)} %all-gather.11.cloned.1.call-done) | copy-start | bytes 25165828
  314.5 5.0 copy-start.31
  319.5 1.2 copy-start.13
  320.2 1.3 copy-start.5
  320.7 1.8 copy-start.17
  321.5 1.0 copy-start.18
  325.1 255.7 %reduce-scatter.5.cloned.1.call-start = ((), (), s32[]{:S(2)}) async-start(), calls=%async_computation.8 | async-start | bytes 6488064 | tf_op jit(solution)/shard_map/reduce_scatter | solution.py:159
  337.1 5.1 copy-start.3
  341.3 1.2 copy-start.6
  341.4 1.5 copy-start.16
  342.9 7.2 copy-start.7
  344.1 1.3 copy-start.12
  346.0 1.2 copy-start.10
  347.3 2.4 copy-start.8
  350.2 1.6 copy-start.20
  358.1 408.3 %reduce-scatter.11.cloned.1.call-start = ((), (), s32[]{:S(2)}) async-start(), calls=%async_computation.11 | async-start | bytes 8650752 | tf_op jit(solution)/shard_map/reduce_scatter | solution.py:159
  371.7 581.2 %reduce-scatter.9.cloned.1.call-start = ((), (), s32[]{:S(2)}) async-start(), calls=%async_computation.10 | async-start | bytes 8650752 | tf_op jit(solution)/shard_map/reduce_scatter | solution.py:159
  393.1 1.3 copy-start.14
  441.3 513.3 %copy-start.1 = (bf16[8,1024]{1,0:T(8,128)(2,1)S(1)}, bf16[8,1024]{1,0:T(8,128)(2,1)}, u32[]{:S(2)}) copy-start(bf16[8,1024]{1,0:T(8,128)(2,1)} %param.19) | copy-start | bytes 49156
Sparse Core Ops, SparseCore 0:
  11.6 72.2 all-gather.6
  87.4 54.8 all-gather.8
  145.9 75.9 all-gather.10
  225.2 75.6 all-gather.12
  325.3 138.3 reduce-scatter.6
  469.2 111.5 reduce-scatter.4
  583.1 183.2 reduce-scatter.10
  768.7 184.0 reduce-scatter.8

commit v2 on v1

--- a/solution.py
+++ b/solution.py
@@ -142,6 +142,13 @@
     return tuple(results)
 
 
+def staged_scatter(member):
+    share = member
+    for name in AXES:
+        share = lax.psum_scatter(share, name, scatter_dimension=0, tiled=True)
+    return share
+
+
 def scatter_all(members):
     devices = lax.psum(1, AXES)
     flat = jnp.concatenate(
@@ -156,9 +163,7 @@
             results.append(summed[start : start + size])
             start += size
         else:
-            share = lax.psum_scatter(
-                member.astype(jnp.bfloat16), AXES, scatter_dimension=0, tiled=True
-            )
+            share = staged_scatter(member.astype(jnp.bfloat16))
             results.append(share.astype(jnp.float32))
     return tuple(results)
 

time: 972 us -> 795 us (0.82)
  waiting for transfers between devices: 662 us -> 484 us
    reduce_scatter x4 -> x12, waiting for transfers between devices: 494 us -> 315 us  [staged_scatter(): share = lax.psum_scatter(share, name, scatter_dimension=0, tiled=True)]
  transfers between devices with their start and end apart: 8 -> 16, of which waited for: 7 -> 11; matrix products, arithmetic and copies ran while one was open for 14% -> 18% of each run, Pallas kernels for 0% -> 0%
where the time goes in v2:
time: 795 us; the launch traced here: 784 us
  waiting for transfers between devices  484 us (61%)
  blocking collectives  111 us (14%)
  matrix products  104 us (13%)
  local copies, waits for them, and re-layouts  39.2 us (5%)
  other arithmetic  28.5 us (4%)
  between operations  16.4 us (2%)
    reduce_scatter x12, waiting for transfers between devices, staged_scatter(): share = lax.psum_scatter(share, name, scatter_dimension=0, tiled=True)  315 us
    all_gather x4, waiting for transfers between devices, gather_all(): results.append(lax.all_gather(member, AXES, axis=0, tiled=True))  168 us
    all_gather x1, blocking collectives, gather_all(): joined = lax.all_gather(flat, AXES, axis=0, tiled=False)  71 us
    unnamed x1, blocking collectives  40.1 us
    dot_general x4, matrix products, cross_rows(): lax.dot_general(former, latter, (((0,), (0,)), ((), ())), preferred_eleme...  31.6 us
    dot_general x4, matrix products, times_transposed(): lax.dot_general(former, latter, (((1,), (1,)), ((), ())), preferred_eleme...  31.5 us
    reshape x8, local copies, waits for them, and re-layouts, split_heads(): return inputs.reshape(inputs.shape[0] // ROW, ROW, HEADS, HEAD_DIM)  25.9 us
  transfers between devices with their start and end apart: 16, of which 11 were waited for; matrix products, arithmetic and copies ran while one was open for 18% of the time, Pallas kernels for 0%

profile of v2, /device:TPU:0, one launch (start us, length us, event | category | flops | bytes accessed | tf_op | source)
XLA Modules:
  0.0 784.1 jit_solution(6225644915686055397)
XLA Ops:
  7.4 1.8 convert_element_type.256
  9.3 1.5 convert_element_type.267
  10.9 1.8 convert_element_type.275
  12.7 0.7 convert_element_type.279
  15.1 71.0 %all-gather.1 = bf16[32,1,384]{2,1,0:T(2,128)(2,1)S(1)} all-gather(bf16[1,1,384]{2,1,0:T(2,128)(2,1)S(1)} %reshape.357), channel_id=2, replica_groups=mesh['dp'=4,'seq'=4,'shard'=2] {'dp','seq','shard'}, dimensions={0}, use_global_device_ids=true | all-gather | bytes 25344 | tf_op jit(solution)/shard_map/all_gather | solution.py:132
  87.7 5.7 fusion.49
  93.6 1.6 fusion.11
  95.2 2.3 reshape.363
  97.5 2.8 copy.68
  100.3 2.3 reshape.364
  102.6 2.8 copy.69
  105.5 4.3 reshape.362
  109.8 3.5 copy.70
  113.3 1.0 fusion.55
  114.3 1.0 fusion.7
  115.4 0.9 copy-done.2
  116.3 0.8 fusion.23
  117.1 1.9 copy.72
  119.1 23.2 %all-gather.9.cloned.1.call-done = bf16[1024,1024]{1,0:T(8,128)(2,1)} async-done(((bf16[32,1024]{1,0:T(8,128)(2,1)}), bf16[1024,1024]{1,0:T(8,128)(2,1)}) %all-gather.9.cloned.1.call-update) | async-done | bytes 2097168 | tf_op jit(solution)/shard_map/all_gather | solution.py:141
  142.3 3.3 fusion.56
  146.0 75.8 %all-gather.11.cloned.1.call-done = bf16[1024,4096]{1,0:T(8,128)(2,1)} async-done(((bf16[32,4096]{1,0:T(8,128)(2,1)}), bf16[1024,4096]{1,0:T(8,128)(2,1)}) %all-gather.11.cloned.1.call-update) | async-done | bytes 8388624 | tf_op jit(solution)/shard_map/all_gather | solution.py:141
  221.8 10.6 %fusion.51 = f32[512,4096]{1,0:T(8,128)} fusion(bf16[1024,4096]{1,0:T(8,128)(2,1)} %all-gather.11.cloned.1.call-done, f32[512,1024]{1,0:T(8,128)S(1)} %get-tuple-element.47, f32[1024]{0:T(1024)S(1)} %reshape.353, f32[1024]{0:T(1024)S(1)} %reshape.352, f32[512]{0:T(512)S(1)} %fusion.46, f32[512]{0:T(512)S(1)} %broadcast_multiply_fusion), kind=kOutput, calls=%fused_computation.125 | convolution fusion | flops 4297588736 | bytes 18886656 | tf_op jit(solution)/shard_map/dot_general | solution.py:224
  232.4 68.5 %all-gather.13.cloned.1.call-done = bf16[4096,1024]{1,0:T(8,128)(2,1)} async-done(((bf16[128,1024]{1,0:T(8,128)(2,1)}), bf16[4096,1024]{1,0:T(8,128)(2,1)}) %all-gather.13.cloned.1.call-update) | async-done | bytes 8388624 | tf_op jit(solution)/shard_map/all_gather | solution.py:141
  301.0 13.5 %convert_reduce_fusion = (f32[4096]{0:T(1024)S(1)}, bf16[512,4096]{1,0:T(8,128)(2,1)S(1)}) fusion(f32[512,4096]{1,0:T(8,128)} %fusion.51, f32[4096]{0:T(1024)S(1)} %fusion.36, bf16[4096,1024]{1,0:T(8,128)(2,1)} %all-gather.13.cloned.1.call-done, bf16[1,512,1024]{2,1,0:T(8,128)(2,1)} %param.22, f32[512]{0:T(512)S(1)} %fusion.41), kind=kOutput, calls=%fused_computation.9 | convolution fusion | flops 4344770560 | bytes 22054912 | tf_op jit(solution)/shard_map/dot_general | solution.py:42
  314.5 5.0 multiply_reduce_fusion.1
  319.5 0.7 fusion.54
  321.5 1.0 copy-done.19
  322.5 2.6 convolution_convert_fusion.3
  325.2 4.2 convolution_convert_fusion.4
  329.4 4.2 reshape.365
  333.6 3.5 copy.74
  337.2 4.2 fusion.24
  341.4 0.9 copy.84
  342.9 1.2 multiply_reduce_fusion
  344.1 1.3 multiply_convert_fusion.1
  345.4 0.7 fusion.27
  346.1 0.9 copy.78
  347.4 1.5 fusion.28
  348.9 0.9 copy.81
  350.3 1.6 copy-done.21
  351.9 6.2 convolution_convert_fusion.2
  358.2 13.5 %convolution_convert_fusion = bf16[4096,1024]{1,0:T(8,128)(2,1)} fusion(bf16[1,512,1024]{2,1,0:T(8,128)(2,1)} %param.22, f32[512]{0:T(512)S(1)} %fusion.41, f32[512,4096]{1,0:T(8,128)} %fusion.51, f32[4096]{0:T(1024)S(1)} %fusion.36), kind=kOutput, calls=%fused_computation.11 | convolution fusion | flops 4321705984 | bytes 17844224 | tf_op jit(solution)/shard_map/dot_general | solution.py:36
  371.8 9.2 %convolution_convert_fusion.1 = bf16[1024,4096]{1,0:T(8,128)(2,1)} fusion(bf16[512,4096]{1,0:T(8,128)(2,1)} %copy-done.34, f32[512,1024]{1,0:T(8,128)S(1)} %get-tuple-element.47, f32[1024]{0:T(1024)S(1)} %reshape.353, f32[1024]{0:T(1024)S(1)} %reshape.352, f32[512]{0:T(512)S(1)} %fusion.46, f32[512]{0:T(512)S(1)} %broadcast_multiply_fusion), kind=kOutput, calls=%fused_computation.12 | convolution fusion | flops 4301783040 | bytes 14692352 | tf_op jit(solution)/shard_map/dot_general | solution.py:36
  381.1 0.7 reduce-scatter.21.cloned.1.call-update
  381.8 34.6 %reduce-scatter.13.cloned.1.call-done = bf16[256,3072]{1,0:T(8,128)(2,1)} async-done(((bf16[1024,3072]{1,0:T(8,128)(2,1)}), bf16[256,3072]{1,0:T(8,128)(2,1)}) %reduce-scatter.13.cloned.1.call-update) | async-done | bytes 1572880 | tf_op jit(solution)/shard_map/reduce_scatter | solution.py:148
  416.4 73.9 %reduce-scatter.31.cloned.1.call-done = bf16[1024,1024]{1,0:T(8,128)(2,1)} async-done(((bf16[4096,1024]{1,0:T(8,128)(2,1)}), bf16[1024,1024]{1,0:T(8,128)(2,1)}) %reduce-scatter.31.cloned.1.call-update) | async-done | bytes 2097168 | tf_op jit(solution)/shard_map/reduce_scatter | solution.py:148
  490.4 74.0 %reduce-scatter.25.cloned.1.call-done = bf16[256,4096]{1,0:T(8,128)(2,1)} async-done(((bf16[1024,4096]{1,0:T(8,128)(2,1)}), bf16[256,4096]{1,0:T(8,128)(2,1)}) %reduce-scatter.25.cloned.1.call-update) | async-done | bytes 2097168 | tf_op jit(solution)/shard_map/reduce_scatter | solution.py:148
  564.5 24.1 %reduce-scatter.21.cloned.1.call-done = bf16[64,1024]{1,0:T(8,128)(2,1)} async-done(((bf16[256,1024]{1,0:T(8,128)(2,1)}), bf16[64,1024]{1,0:T(8,128)(2,1)}) %reduce-scatter.21.cloned.1.call-update) | async-done | bytes 131088 | tf_op jit(solution)/shard_map/reduce_scatter | solution.py:148
  588.7 1.5 fusion.15
  590.3 34.1 %reduce-scatter.15.cloned.1.call-done = bf16[64,3072]{1,0:T(8,128)(2,1)} async-done(((bf16[256,3072]{1,0:T(8,128)(2,1)}), bf16[64,3072]{1,0:T(8,128)(2,1)}) %reduce-scatter.15.cloned.1.call-update) | async-done | bytes 393232 | tf_op jit(solution)/shard_map/reduce_scatter | solution.py:148
  624.8 12.2 %fusion.29 = bf16[1,512,1024]{2,1,0:T(8,128)(2,1)} fusion(f32[512,1024]{1,0:T(8,128)S(1)} %get-tuple-element.47, bf16[4096,1024]{1,0:T(8,128)(2,1)} %all-gather.13.cloned.1.call-done, f32[1024]{0:T(1024)S(1)} %reshape.355, f32[512,4096]{1,0:T(8,128)} %fusion.51, f32[4096]{0:T(1024)S(1)} %fusion.36), kind=kOutput, calls=%fused_computation.65 | convolution fusion | flops 4317511680 | bytes 19943424 | tf_op jit(solution)/shard_map/dot_general | solution.py:228
  637.0 32.3 %reduce-scatter.33.cloned.1.call-done = bf16[256,1024]{1,0:T(8,128)(2,1)} async-done(((bf16[1024,1024]{1,0:T(8,128)(2,1)}), bf16[256,1024]{1,0:T(8,128)(2,1)}) %reduce-scatter.33.cloned.1.call-update) | async-done | bytes 524304 | tf_op jit(solution)/shard_map/reduce_scatter | solution.py:148
  669.3 8.9 %fusion.52 = (f32[1024]{0:T(1024)S(1)}, f32[512]{0:T(512)S(1)}, f32[512,1024]{1,0:T(8,128)}) fusion(f32[1024]{0:T(1024)S(1)} %reshape.347, f32[512]{0:T(512)S(1)} %broadcast_multiply_fusion.1, f32[1024]{0:T(1024)S(1)} %bitcast.154, bf16[1,512,1024]{2,1,0:T(8,128)(2,1)S(1)} %copy-done.4, bf16[512,3072]{0,1:T(8,128)(2,1)} %copy-done.21, ...), kind=kOutput, calls=%fused_computation.126 | convolution fusion | flops 3224893952 | bytes 12599296 | tf_op jit(solution)/shard_map/dot_general | solution.py:42
  678.8 2.7 multiply_reduce_fusion.2
  681.5 32.8 %reduce-scatter.27.cloned.1.call-done = bf16[64,4096]{1,0:T(8,128)(2,1)} async-done(((bf16[256,4096]{1,0:T(8,128)(2,1)}), bf16[64,4096]{1,0:T(8,128)(2,1)}) %reduce-scatter.27.cloned.1.call-update) | async-done | bytes 524304 | tf_op jit(solution)/shard_map/reduce_scatter | solution.py:148
  714.3 1.4 convert_reduce_fusion.3
  716.0 40.1 %all-reduce = f32[32,384]{1,0:T(8,128)S(1)} all-reduce(f32[32,384]{1,0:T(8,128)S(1)} %concatenate.12), channel_id=3, replica_groups=mesh['dp'=4,'seq'=4,'shard'=2] {'dp','seq','shard'}, use_global_device_ids=true, to_apply=%region_20.21.clone | all-reduce | flops 12288 | bytes 98304
  756.7 0.6 dynamic-slice_bitcast_fusion
  757.3 3.6 add_bitcast_fusion
  760.9 1.5 convert_element_type.298
  762.4 1.7 convert_element_type.296
  764.1 1.8 convert_element_type.302
  765.9 9.4 %reduce-scatter.29.cloned.1.call-done = bf16[32,4096]{1,0:T(8,128)(2,1)} async-done(((bf16[64,4096]{1,0:T(8,128)(2,1)}), bf16[32,4096]{1,0:T(8,128)(2,1)}) %reduce-scatter.29.cloned.1.call-update) | async-done | bytes 262160 | tf_op jit(solution)/shard_map/reduce_scatter | solution.py:148
  775.4 1.8 convert_element_type.300
  (156 shorter events, 7.9 us)
Async XLA Ops:
  7.2 79.6 %copy-start = (bf16[8,1024]{1,0:T(8,128)(2,1)S(1)}, bf16[8,1024]{1,0:T(8,128)(2,1)}, u32[]{:S(2)}) copy-start(bf16[8,1024]{1,0:T(8,128)(2,1)} %param.19) | copy-start | bytes 49156
  7.2 5.5 copy-start.20
  7.2 7.6 copy-start.25
  7.2 7.6 copy-start.26
  7.2 7.7 copy-start.27
  7.2 7.7 copy-start.28
  7.3 7.7 copy-start.29
  7.3 7.7 copy-start.30
  7.3 7.7 copy-start.31
  7.3 7.7 copy-start.32
  7.3 7.7 copy-start.33
  7.3 79.6 %copy-start.4 = (bf16[1,512,1024]{2,1,0:T(8,128)(2,1)S(1)}, bf16[1,512,1024]{2,1,0:T(8,128)(2,1)}, u32[]{:S(2)}) copy-start(bf16[1,512,1024]{2,1,0:T(8,128)(2,1)} %param.18) | copy-start | bytes 3145732
  7.3 80.4 %all-gather.7.cloned.1.call-start = ((), (), s32[]{:S(2)}) async-start(), calls=%async_computation.12 | async-start | bytes 6488064 | tf_op jit(solution)/shard_map/all_gather | solution.py:141
  9.2 133.1 %all-gather.9.cloned.1.call-start = ((), (), s32[]{:S(2)}) async-start(), calls=%async_computation.13 | async-start | bytes 2162688 | tf_op jit(solution)/shard_map/all_gather | solution.py:141
  10.8 211.0 %all-gather.11.cloned.1.call-start = ((), (), s32[]{:S(2)}) async-start(), calls=%async_computation.14 | async-start | bytes 8650752 | tf_op jit(solution)/shard_map/all_gather | solution.py:141
  12.7 288.3 %all-gather.13.cloned.1.call-start = ((), (), s32[]{:S(2)}) async-start(), calls=%async_computation.15 | async-start | bytes 8650752 | tf_op jit(solution)/shard_map/all_gather | solution.py:141
  13.5 367.6 %reduce-scatter.19.cloned.1.call-start = ((), (), s32[]{:S(2)}) async-start(), calls=%async_computation.19 | async-start | bytes 2621440 | tf_op jit(solution)/shard_map/reduce_scatter | solution.py:148
  87.6 5.8 copy-start.22
  100.3 13.0 %copy-start.11 = (bf16[4,128,16,64]{1,3,2,0:T(8,128)(2,1)}, bf16[4,128,16,64]{1,3,2,0:T(8,128)(2,1)S(1)}, u32[]{:S(2)}) copy-start(bf16[4,128,16,64]{1,3,2,0:T(8,128)(2,1)S(1)} %copy.68) | copy-start | bytes 3145732
  105.5 7.9 %copy-start.13 = (bf16[4,128,16,64]{1,3,2,0:T(8,128)(2,1)}, bf16[4,128,16,64]{1,3,2,0:T(8,128)(2,1)S(1)}, u32[]{:S(2)}) copy-start(bf16[4,128,16,64]{1,3,2,0:T(8,128)(2,1)S(1)} %copy.69) | copy-start | bytes 3145732
  114.3 2.0 copy-start.2
  114.3 2.0 copy-start.16
  301.0 13.5 %copy-start.24 = (bf16[1024,4096]{1,0:T(8,128)(2,1)S(1)}, bf16[1024,4096]{1,0:T(8,128)(2,1)}, u32[]{:S(2)}) copy-start(bf16[1024,4096]{1,0:T(8,128)(2,1)} %all-gather.11.cloned.1.call-done) | copy-start | bytes 25165828
  314.5 5.0 copy-start.34
  319.5 1.2 copy-start.15
  320.2 1.3 copy-start.5
  320.7 1.8 copy-start.18
  321.5 1.0 copy-start.19
  325.1 91.2 %reduce-scatter.13.cloned.1.call-start = ((), (), s32[]{:S(2)}) async-start(), calls=%async_computation.16 | async-start | bytes 7864320 | tf_op jit(solution)/shard_map/reduce_scatter | solution.py:148
  337.2 5.1 copy-start.3
  341.4 1.2 copy-start.7
  341.4 1.5 copy-start.17
  342.9 7.2 copy-start.9
  344.1 1.3 copy-start.14
  346.1 1.2 copy-start.12
  347.3 2.4 copy-start.8
  350.3 1.6 copy-start.21
  358.2 132.2 %reduce-scatter.31.cloned.1.call-start = ((), (), s32[]{:S(2)}) async-start(), calls=%async_computation.25 | async-start | bytes 10485760 | tf_op jit(solution)/shard_map/reduce_scatter | solution.py:148
  371.7 192.7 %reduce-scatter.25.cloned.1.call-start = ((), (), s32[]{:S(2)}) async-start(), calls=%async_computation.22 | async-start | bytes 10485760 | tf_op jit(solution)/shard_map/reduce_scatter | solution.py:148
  381.0 207.6 %reduce-scatter.21.cloned.1.call-start = ((), (), s32[]{:S(2)}) async-start(), calls=%async_computation.20 | async-start | bytes 655360 | tf_op jit(solution)/shard_map/reduce_scatter | solution.py:148
  381.7 242.7 %reduce-scatter.15.cloned.1.call-start = ((), (), s32[]{:S(2)}) async-start(), calls=%async_computation.17 | async-start | bytes 1966080 | tf_op jit(solution)/shard_map/reduce_scatter | solution.py:148
  416.4 252.9 %reduce-scatter.33.cloned.1.call-start = ((), (), s32[]{:S(2)}) async-start(), calls=%async_computation.26 | async-start | bytes 2621440 | tf_op jit(solution)/shard_map/reduce_scatter | solution.py:148
  490.4 223.9 %reduce-scatter.27.cloned.1.call-start = ((), (), s32[]{:S(2)}) async-start(), calls=%async_computation.23 | async-start | bytes 2621440 | tf_op jit(solution)/shard_map/reduce_scatter | solution.py:148
  564.4 196.5 %reduce-scatter.23.cloned.1.call-start = ((), (), s32[]{:S(2)}) async-start(), calls=%async_computation.21 | async-start | bytes 196608 | tf_op jit(solution)/shard_map/reduce_scatter | solution.py:148
  588.6 173.8 %reduce-scatter.17.cloned.1.call-start = ((), (), s32[]{:S(2)}) async-start(), calls=%async_computation.18 | async-start | bytes 589824 | tf_op jit(solution)/shard_map/reduce_scatter | solution.py:148
  624.5 139.7 %reduce-scatter.35.cloned.1.call-start = ((), (), s32[]{:S(2)}) async-start(), calls=%async_computation.27 | async-start | bytes 786432 | tf_op jit(solution)/shard_map/reduce_scatter | solution.py:148
  669.3 9.1 %copy-start.10 = (bf16[4,128,16,64]{1,0,3,2:T(4,128)(2,1)S(1)}, bf16[4,128,16,64]{1,0,3,2:T(4,128)(2,1)}, u32[]{:S(2)}) copy-start(bf16[4,128,16,64]{1,0,3,2:T(4,128)(2,1)} %copy-done.9) | copy-start | bytes 3145732
  669.3 9.4 %copy-start.23 = (f32[512]{0:T(512)S(1)}, f32[512]{0:T(512)}, u32[]{:S(2)}) copy-start(f32[512]{0:T(512)} %copy-done.22) | copy-start | bytes 6148
  669.3 106.1 %reduce-scatter.29.cloned.1.call-start = ((), (), s32[]{:S(2)}) async-start(), calls=%async_computation.24 | async-start | bytes 786432 | tf_op jit(solution)/shard_map/reduce_scatter | solution.py:148
  678.7 78.6 %copy-start.6 = (f32[512,1024]{1,0:T(8,128)S(1)}, f32[512,1024]{1,0:T(8,128)}, u32[]{:S(2)}) copy-start(f32[512,1024]{1,0:T(8,128)} %copy-done.5) | copy-start | bytes 6291460
  757.3 19.8 %copy-start.1 = (bf16[8,1024]{1,0:T(8,128)(2,1)S(1)}, bf16[8,1024]{1,0:T(8,128)(2,1)}, u32[]{:S(2)}) copy-start(bf16[8,1024]{1,0:T(8,128)(2,1)} %param.19) | copy-start | bytes 49156
Sparse Core Ops, SparseCore 0:
  11.6 72.2 all-gather.6
  87.4 54.8 all-gather.8
  145.9 75.9 all-gather.10
  225.2 75.6 all-gather.12
  325.3 29.7 reduce-scatter.18
  358.3 58.0 reduce-scatter.12
  418.9 71.3 reduce-scatter.30
  492.9 71.4 reduce-scatter.24
  566.7 21.8 reduce-scatter.20
  590.7 33.6 reduce-scatter.14
  626.8 42.4 reduce-scatter.32
  671.4 42.8 reduce-scatter.26
  716.5 9.8 reduce-scatter.22
  728.5 12.9 reduce-scatter.16
  743.6 15.1 reduce-scatter.34
  760.9 14.4 reduce-scatter.28
